TPU v7x, 32 devices: a whole 2x2x4 slice. The times are simulated.
32 devices in a mesh: row: 8 (over z, y), col: 4 (over x, core).
Axes of the slice: x: 2, y: 2, z: 4, core: 2. Of those that a mesh axis runs over, the one named last changes fastest.
Arguments:
- inv_blocks: bfloat16 [2048, 2048], P('row', 'col'), may hold values from -0.125 to 0.125
- factor: bfloat16 [4, 2048, 128], P('col', 'row'), may hold values from -2.3125 to 2.3125
- pattern: int32 [4, 16], P('col', 'row'), may hold values from 0 to 1, as said below
- diag_inv: float32 [4, 128, 128], P(None, 'row', 'col'), may hold values from -12 to 12
Outputs:
- inverse_panel: bfloat16 [4, 128, 2048], P(None, 'col', 'row')
- diag_block: float32 [4, 128, 128], P(None, 'row', 'col')
Inputs may be any that keep to these rules, and one draw needn't show every extreme that they name: pattern is 0 or 1; each supernode has its own share of 1s.
All inputs are finite; a program needn't handle non-finite values.
Results may differ from a plain program's by a relative error of at most 0.0005.
Values may be sent and summed in bfloat16 or wider, within the bound.
No kernel may reach another device: no remote copies, remote signals or barrier semaphores. Data moves between devices by JAX's collectives and lax.ppermute only.
A program may use at most 64 MiB of HBM per device.

v0:
```python
import jax
import jax.numpy as jnp
from jax import lax
from jax.sharding import PartitionSpec as P


def broadcast(block, axis, owner):
    block = jnp.where(lax.axis_index(axis) == owner, block, jnp.zeros_like(block))
    return lax.psum(block, axis)


def on_device(inv_blocks, factor, pattern, diag_inv):
    width = factor.shape[2]
    n_row = lax.axis_size("row")
    n_col = lax.axis_size("col")
    ratio = n_row // n_col
    col_place = lax.axis_index("col")
    row_place = lax.axis_index("row")
    keep = jnp.repeat(pattern, width, axis=1).astype(jnp.bfloat16)
    own_masked = factor * keep[:, :, None]
    level_rows = lax.all_gather(own_masked, "col", axis=0, tiled=True)
    pieces = []
    for offset in range(ratio):
        pieces.append(broadcast(level_rows, "row", col_place * ratio + offset))
    column_rows = jnp.concatenate(pieces, axis=1)
    level_float = level_rows.astype(jnp.float32)
    row_span = width // n_row
    share = lax.psum_scatter(
        -jnp.einsum("ij,sjw->wsi", inv_blocks, column_rows, preferred_element_type=jnp.float32),
        "col",
        scatter_dimension=0,
        tiled=True,
    )
    inner = jnp.einsum("siw,vsi->swv", level_float, share, precision=lax.Precision.HIGHEST)
    inner_total = lax.psum(inner, "row")
    inner_sum = lax.dynamic_slice_in_dim(inner_total, row_place * row_span, row_span, 1)
    inverse_panel = jnp.transpose(share, (1, 0, 2)).astype(jnp.bfloat16)
    return (inverse_panel, diag_inv - inner_sum)


def solution(mesh):
    return jax.shard_map(
        on_device,
        mesh=mesh,
        in_specs=(P("row", "col"), P("col", "row", None), P("col", "row"), P(None, "row", "col")),
        out_specs=(P(None, "col", "row"), P(None, "row", "col")),
        check_vma=False,
    )
```

profile of v0, /device:TPU:0, one launch (start us, length us, event | category | flops | bytes accessed | tf_op | source)
XLA Modules:
  0.0 197.1 jit_solution(16191956537070518140)
XLA Ops:
  7.2 0.0 copy-start
  7.2 0.0 all-reduce.6.cloned.1.call-start
  7.2 0.0 copy-start.3
  7.2 0.7 copy-done.3
  7.9 0.1 broadcast_bitcast_fusion
  8.0 0.9 broadcast_multiply_fusion
  8.9 7.2 %all_gather.3 = bf16[4,256,128]{2,1,0:T(8,128)(2,1)S(1)} all-gather(bf16[1,256,128]{2,1,0:T(8,128)(2,1)S(1)} %broadcast_multiply_fusion), channel_id=1, replica_groups=mesh['row'=8,'col'=4] {'col'}, dimensions={0}, use_global_device_ids=true | all-gather | bytes 327680 | tf_op jit(solution)/shard_map/all_gather | solution.py:21
  16.2 0.1 copy.7
  16.3 0.8 broadcast_select_fusion.1
  17.2 0.0 all-reduce.6.cloned.1.call-update
  17.2 0.0 reduce-scatter.2.cloned.1.call-start
  17.2 74.1 %all-reduce.6.cloned.1.call-done = (bf16[4,256,128]{1,2,0:T(8,128)(2,1)}, bf16[4,256,128]{1,2,0:T(8,128)(2,1)}) async-done(((bf16[4,256,128]{1,2,0:T(8,128)(2,1)}, bf16[4,256,128]{1,2,0:T(8,128)(2,1)}), (bf16[4,256,128]{1,2,0:T(8,128)(2,1)}, bf16[4,256,128]{1,2,0:T(8,128)(2,1)})) %all-reduce.6.cloned.1.call-update) | async-done | bytes 524304 | tf_op jit(solution)/shard_map/psum | solution.py:9
  91.4 0.0 copy-done
  91.4 2.1 %fusion = f32[128,4,256]{2,0,1:T(8,128)} fusion(bf16[4,256,128]{1,2,0:T(8,128)(2,1)} %get-tuple-element.2, bf16[4,256,128]{1,2,0:T(8,128)(2,1)} %get-tuple-element.3, bf16[256,512]{1,0:T(8,128)(2,1)S(1)} %copy-done), kind=kOutput, calls=%fused_computation.1 | convolution fusion | flops 135397376 | bytes 1310720 | tf_op jit(solution)/shard_map/ij,sjw->wsi/dot_general | solution.py:29
  93.5 0.0 reduce-scatter.2.cloned.1.call-update
  93.5 0.0 all-reduce.4.cloned.1.call-start
  93.6 21.1 %reduce-scatter.2.cloned.1.call-done = f32[32,4,256]{2,0,1:T(8,128)} async-done(((f32[128,4,256]{2,0,1:T(8,128)}), f32[32,4,256]{2,0,1:T(8,128)}) %reduce-scatter.2.cloned.1.call-update) | async-done | bytes 131088 | tf_op jit(solution)/shard_map/reduce_scatter | solution.py:28
  114.7 2.0 %fusion.6 = f32[4,128,32]{2,1,0:T(8,128)} fusion(bf16[4,256,128]{2,1,0:T(8,128)(2,1)S(1)} %all_gather.3, f32[32,4,256]{2,0,1:T(8,128)} %reduce-scatter.2.cloned.1.call-done), kind=kOutput, calls=%fused_computation.14 | convolution fusion | flops 50331648 | bytes 458752 | tf_op jit(solution)/shard_map/siw,vsi->swv/dot_general | solution.py:34
  116.7 0.0 copy-start.1
  116.7 0.0 all-reduce.4.cloned.1.call-update
  116.8 0.9 copy-done.1
  117.6 0.0 copy-start.2
  117.7 0.6 convert_bitcast_fusion
  118.3 70.9 %all-reduce.4.cloned.1.call-done = f32[4,128,32]{2,1,0:T(8,128)} async-done(((f32[4,128,32]{2,1,0:T(8,128)}), f32[4,128,32]{2,1,0:T(8,128)}) %all-reduce.4.cloned.1.call-update) | async-done | bytes 65552 | tf_op jit(solution)/shard_map/psum | solution.py:35
  189.2 0.0 copy-done.2
  189.2 1.4 dynamic-slice_subtract_fusion
  (1 shorter events, 0.0 us)
Async XLA Ops:
  7.2 84.2 %copy-start = (bf16[256,512]{1,0:T(8,128)(2,1)S(1)}, bf16[256,512]{1,0:T(8,128)(2,1)}, u32[]{:S(2)}) copy-start(bf16[256,512]{1,0:T(8,128)(2,1)} %param.4) | copy-start | bytes 786436
  7.2 84.2 %all-reduce.6.cloned.1.call-start = ((), (), s32[]{:S(2)}) async-start(), calls=%async_computation.3 | async-start | bytes 1048576 | tf_op jit(solution)/shard_map/psum | solution.py:9
  7.2 0.7 copy-start.3
  17.2 97.6 %reduce-scatter.2.cloned.1.call-start = ((), (), s32[]{:S(2)}) async-start(), calls=%async_computation.1 | async-start | bytes 655360 | tf_op jit(solution)/shard_map/reduce_scatter | solution.py:28
  93.5 95.6 %all-reduce.4.cloned.1.call-start = ((), (), s32[]{:S(2)}) async-start(), calls=%async_computation.2 | async-start | bytes 524288 | tf_op jit(solution)/shard_map/psum | solution.py:35
  116.7 0.9 copy-start.1
  117.6 71.5 %copy-start.2 = (f32[4,16,32]{2,1,0:T(8,128)S(1)}, f32[4,16,32]{2,1,0:T(8,128)}, u32[]{:S(2)}) copy-start(f32[4,16,32]{2,1,0:T(8,128)} %param.7) | copy-start | bytes 24580
Sparse Core Ops, SparseCore 0:
  17.3 74.0 all-reduce.5
  93.9 20.8 reduce-scatter.1
  118.1 71.0 all-reduce.3
where the time goes:
time: 197 us
  waiting for transfers between devices  166 us (84%)
  between operations  13.8 us (7%)
  blocking collectives  7.22 us (4%)
  matrix products  4.16 us (2%)
  other arithmetic  3.79 us (2%)
    psum x1, waiting for transfers between devices, broadcast(): return lax.psum(block, axis)  74.1 us
    psum x1, waiting for transfers between devices, on_device(): inner_total = lax.psum(inner, 'row')  70.9 us
    reduce_scatter x1, waiting for transfers between devices, on_device(): lax.psum_scatter(-jnp.einsum('ij,sjw->wsi', inv_blocks, column_rows, pref...  21.1 us
    all_gather x1, blocking collectives, on_device(): level_rows = lax.all_gather(own_masked, 'col', axis=0, tiled=True)  7.22 us
  transfers between devices with their start and end apart: 3, of which 3 were waited for; matrix products, arithmetic and copies ran while one was open for 0% of the time, Pallas kernels for 0%

commit v1 on v0

--- a/solution.py
+++ b/solution.py
@@ -4,9 +4,15 @@
 from jax.sharding import PartitionSpec as P
 
 
+def summed_here(x, axis):
+    shards = lax.all_gather(x, axis, axis=0, tiled=False)
+    total = shards.sum(axis=0)
+    return total
+
+
 def broadcast(block, axis, owner):
     block = jnp.where(lax.axis_index(axis) == owner, block, jnp.zeros_like(block))
-    return lax.psum(block, axis)
+    return summed_here(block, axis)
 
 
 def on_device(inv_blocks, factor, pattern, diag_inv):

time: 197 us -> 223 us (1.13)
  waiting for transfers between devices: 166 us -> 189 us
  other arithmetic: 3.79 us -> 9.23 us
    all_gather x0 -> x2, waiting for transfers between devices: none -> 97.4 us  [summed_here(): shards = lax.all_gather(x, axis, axis=0, tiled=False)]
    psum x1 -> x0, waiting for transfers between devices: 74.1 us -> none  [broadcast(): return lax.psum(block, axis)]
    reduce_sum x0 -> x2, other arithmetic: none -> 3.85 us  [summed_here(): total = shards.sum(axis=0)]
  transfers between devices with their start and end apart: 3 -> 4, of which waited for: 3 -> 4; matrix products, arithmetic and copies ran while one was open for 0% -> 2% of each run, Pallas kernels for 0% -> 0%
where the time goes in v1:
time: 223 us
  waiting for transfers between devices  189 us (85%)
  between operations  13.8 us (6%)
  other arithmetic  9.23 us (4%)
  blocking collectives  7.22 us (3%)
  matrix products  3.14 us (1%)
    all_gather x2, waiting for transfers between devices, summed_here(): shards = lax.all_gather(x, axis, axis=0, tiled=False)  97.4 us
    psum x1, waiting for transfers between devices, on_device(): inner_total = lax.psum(inner, 'row')  70.7 us
    reduce_scatter x1, waiting for transfers between devices, on_device(): lax.psum_scatter(-jnp.einsum('ij,sjw->wsi', inv_blocks, column_rows, pref...  20.3 us
    all_gather x1, blocking collectives, on_device(): level_rows = lax.all_gather(own_masked, 'col', axis=0, tiled=True)  7.22 us
  transfers between devices with their start and end apart: 4, of which 4 were waited for; matrix products, arithmetic and copies ran while one was open for 2% of the time, Pallas kernels for 0%

profile of v1, /device:TPU:0, one launch (start us, length us, event | category | flops | bytes accessed | tf_op | source)
XLA Modules:
  0.0 223.1 jit_solution(18065638594800699683)
XLA Ops:
  7.2 0.0 copy-start
  7.2 0.0 all-gather.5.cloned.1.call-start
  7.2 0.7 convert_bitcast_fusion.1
  7.9 0.1 broadcast_bitcast_fusion
  8.0 0.9 broadcast_multiply_fusion
  8.9 7.2 %all_gather.15 = bf16[4,256,128]{2,1,0:T(8,128)(2,1)S(1)} all-gather(bf16[1,256,128]{2,1,0:T(8,128)(2,1)S(1)} %broadcast_multiply_fusion), channel_id=1, replica_groups=mesh['row'=8,'col'=4] {'col'}, dimensions={0}, use_global_device_ids=true | all-gather | bytes 327680 | tf_op jit(solution)/shard_map/all_gather | solution.py:27
  16.2 0.8 broadcast_select_fusion.1
  17.0 0.0 all-gather.5.cloned.1.call-update
  17.0 0.0 all-gather.7.cloned.1.call-start
  17.1 0.7 all-gather.7.cloned.1.call-update
  17.8 0.0 reduce-scatter.2.cloned.1.call-start
  17.8 49.7 %all-gather.5.cloned.1.call-done = bf16[32,256,128]{2,1,0:T(8,128)(2,1)} async-done(((bf16[4,256,128]{2,1,0:T(8,128)(2,1)}), bf16[32,256,128]{2,1,0:T(8,128)(2,1)}) %all-gather.5.cloned.1.call-update) | async-done | bytes 2097168 | tf_op jit(solution)/shard_map/all_gather | solution.py:8
  67.6 1.9 reduce_sum.24
  69.5 0.1 copy.8
  69.6 47.7 %all-gather.7.cloned.1.call-done = bf16[32,256,128]{2,1,0:T(8,128)(2,1)} async-done(((bf16[4,256,128]{2,1,0:T(8,128)(2,1)}), bf16[32,256,128]{2,1,0:T(8,128)(2,1)}) %all-gather.7.cloned.1.call-update) | async-done | bytes 2097168 | tf_op jit(solution)/shard_map/all_gather | solution.py:8
  117.3 1.9 reduce_sum.25
  119.3 0.0 copy-start.1
  119.3 0.1 copy.9
  119.4 0.0 copy-done
  119.4 1.1 fusion
  120.6 0.0 reduce-scatter.2.cloned.1.call-update
  120.6 0.0 all-reduce.2.cloned.1.call-start
  120.6 20.3 %reduce-scatter.2.cloned.1.call-done = f32[32,4,256]{2,0,1:T(8,128)} async-done(((f32[128,4,256]{2,0,1:T(8,128)}), f32[32,4,256]{2,0,1:T(8,128)}) %reduce-scatter.2.cloned.1.call-update) | async-done | bytes 131088 | tf_op jit(solution)/shard_map/reduce_scatter | solution.py:34
  140.9 2.0 fusion.6
  142.9 0.0 all-reduce.2.cloned.1.call-update
  143.0 1.5 convert_bitcast_fusion
  144.5 70.7 %all-reduce.2.cloned.1.call-done = f32[4,128,32]{2,1,0:T(8,128)} async-done(((f32[4,128,32]{2,1,0:T(8,128)}), f32[4,128,32]{2,1,0:T(8,128)}) %all-reduce.2.cloned.1.call-update) | async-done | bytes 65552 | tf_op jit(solution)/shard_map/psum | solution.py:41
  215.2 0.0 copy-done.1
  215.2 1.4 dynamic-slice_subtract_fusion
Async XLA Ops:
  7.2 112.3 %copy-start = (bf16[256,512]{1,0:T(8,128)(2,1)S(1)}, bf16[256,512]{1,0:T(8,128)(2,1)}, u32[]{:S(2)}) copy-start(bf16[256,512]{1,0:T(8,128)(2,1)} %param.4) | copy-start | bytes 786436
  7.2 60.4 %all-gather.5.cloned.1.call-start = ((), (), s32[]{:S(2)}) async-start(), calls=%async_computation.3 | async-start | bytes 2359296 | tf_op jit(solution)/shard_map/all_gather | solution.py:8
  17.0 100.3 %all-gather.7.cloned.1.call-start = ((), (), s32[]{:S(2)}) async-start(), calls=%async_computation.4 | async-start | bytes 2359296 | tf_op jit(solution)/shard_map/all_gather | solution.py:8
  17.8 123.1 %reduce-scatter.2.cloned.1.call-start = ((), (), s32[]{:S(2)}) async-start(), calls=%async_computation.1 | async-start | bytes 655360 | tf_op jit(solution)/shard_map/reduce_scatter | solution.py:34
  119.3 95.9 %copy-start.1 = (f32[4,16,32]{2,1,0:T(8,128)S(1)}, f32[4,16,32]{2,1,0:T(8,128)}, u32[]{:S(2)}) copy-start(f32[4,16,32]{2,1,0:T(8,128)} %param.7) | copy-start | bytes 24580
  120.6 94.6 %all-reduce.2.cloned.1.call-start = ((), (), s32[]{:S(2)}) async-start(), calls=%async_computation.2 | async-start | bytes 524288 | tf_op jit(solution)/shard_map/psum | solution.py:41
Sparse Core Ops, SparseCore 0:
  17.2 50.3 all-gather.4
  69.7 47.6 all-gather.6
  120.7 20.1 reduce-scatter.1
  144.1 71.0 all-reduce.1
